TPU v7x, 32 devices: a whole 2x2x4 slice. The times are simulated.
32 devices in a mesh: row: 8 (over z, y), col: 4 (over x, core).
Axes of the slice: x: 2, y: 2, z: 4, core: 2. Of those that a mesh axis runs over, the one named last changes fastest.
Arguments:
- layer_input: bfloat16 [1024, 12288], P(None, 'row'), may hold values from -6 to 6
- hidden_pre: bfloat16 [1024, 24576], P(None, 'col'), may hold values from -6 to 6
- out_grad: bfloat16 [1024, 12288], P(None, 'row'), may hold values from -8 to 8
- w_up: bfloat16 [12288, 24576], P('row', 'col'), may hold values from -0.0546875 to 0.0546875
- w_down: bfloat16 [24576, 12288], P('col', 'row'), may hold values from -0.0390625 to 0.0390625
Outputs:
- in_grad: bfloat16 [1024, 12288], P('col', 'row')
- up_grad: bfloat16 [12288, 24576], P('row', 'col')
- down_grad: bfloat16 [24576, 12288], P('col', 'row')
All inputs are finite; a program needn't handle non-finite values.
Results may differ from a plain program's by a relative error of at most 0.0051.
Values may be sent and summed in bfloat16 or wider, within the bound.
A program may use at most 320 MiB of HBM per device.

v0:
```python
import math
import jax
import jax.numpy as jnp
from jax import lax
from jax.sharding import PartitionSpec as P

GELU_COEF = 0.7978845608
CUBIC_COEF = 0.044715
CONTRACT_LAST = (((1,), (1,)), ((), ()))
CONTRACT_FIRST = (((0,), (0,)), ((), ()))


def gelu_value(pre_act):
    inner = GELU_COEF * (pre_act + CUBIC_COEF * pre_act * pre_act * pre_act)
    return 0.5 * pre_act * (1.0 + jnp.tanh(inner))


def gelu_slope(pre_act):
    inner = GELU_COEF * (pre_act + CUBIC_COEF * pre_act * pre_act * pre_act)
    tangent = jnp.tanh(inner)
    return 0.5 * (1.0 + tangent) + 0.5 * pre_act * (1.0 - tangent * tangent) * GELU_COEF * (
        1.0 + 3.0 * CUBIC_COEF * pre_act * pre_act
    )


def body(layer_input, hidden_pre, out_grad, w_up, w_down):
    token_count = out_grad.shape[0]
    scaling = 1.0 / math.sqrt(token_count)
    pre_act = hidden_pre.astype(jnp.float32)
    activated = gelu_value(pre_act).astype(jnp.bfloat16)
    down_total = lax.dot_general(
        activated, out_grad, CONTRACT_FIRST, preferred_element_type=jnp.float32
    )
    down_grad = (down_total * scaling).astype(jnp.bfloat16)
    local_sum = lax.dot_general(out_grad, w_down, CONTRACT_LAST, preferred_element_type=jnp.float32)
    summed = lax.psum(local_sum, "row")
    hidden_grad = (summed * gelu_slope(pre_act)).astype(jnp.bfloat16)
    up_total = lax.dot_general(
        layer_input, hidden_grad, CONTRACT_FIRST, preferred_element_type=jnp.float32
    )
    in_partial = lax.dot_general(
        hidden_grad, w_up, CONTRACT_LAST, preferred_element_type=jnp.float32
    )
    up_grad = (up_total * scaling).astype(jnp.bfloat16)
    in_grad = lax.psum_scatter(in_partial, "col", scatter_dimension=0, tiled=True).astype(
        jnp.bfloat16
    )
    return (in_grad, up_grad, down_grad)


def solution(mesh):
    placed = (P(None, "row"), P(None, "col"), P(None, "row"), P("row", "col"), P("col", "row"))
    return jax.shard_map(
        body,
        mesh=mesh,
        in_specs=placed,
        out_specs=(P("col", "row"), P("row", "col"), P("col", "row")),
        check_vma=False,
    )
```

profile of v0, /device:TPU:0, one launch (start us, length us, event | category | flops | bytes accessed | tf_op | source)
XLA Modules:
  0.0 922.6 jit_solution(7426446463446432995)
XLA Ops:
  7.2 0.0 copy-start
  7.2 0.0 all-reduce.2.cloned.1.call-start
  7.2 1.8 copy-done
  9.1 25.3 %fusion.21 = f32[1024,6144]{1,0:T(8,128)} fusion(bf16[1024,1536]{1,0:T(8,128)(2,1)S(1)} %copy-done, bf16[6144,1536]{1,0:T(8,128)(2,1)} %param.9), kind=kOutput, calls=%fused_computation.29 | convolution fusion | flops 19327352832 | bytes 47185920 | tf_op jit(solution)/shard_map/dot_general | solution.py:35
  34.4 0.0 all-reduce.2.cloned.1.call-update
  34.4 0.0 reduce-scatter.2.cloned.1.call-start
  34.5 745.5 %all-reduce.2.cloned.1.call-done = f32[1024,6144]{1,0:T(8,128)} async-done(((f32[1024,6144]{1,0:T(8,128)}), f32[1024,6144]{1,0:T(8,128)}) %all-reduce.2.cloned.1.call-update) | async-done | bytes 25165840 | tf_op jit(solution)/shard_map/psum | solution.py:36
  780.0 19.7 %fusion.6 = bf16[1024,6144]{1,0:T(8,128)(2,1)S(1)} fusion(f32[1024,6144]{1,0:T(8,128)} %all-reduce.2.cloned.1.call-done, bf16[1024,6144]{1,0:T(8,128)(2,1)} %param.6), kind=kLoop, calls=%fused_computation.15 | loop fusion | flops 125829120 | bytes 50331648 | tf_op jit(solution)/shard_map/convert_element_type | solution.py:37
  799.8 0.0 copy-start.1
  799.8 4.8 copy-done.1
  804.5 24.3 %fusion.22 = f32[1024,1536]{1,0:T(8,128)} fusion(bf16[1024,6144]{1,0:T(8,128)(2,1)S(1)} %fusion.6, bf16[1536,6144]{1,0:T(8,128)(2,1)} %param.8), kind=kOutput, calls=%fused_computation.30 | convolution fusion | flops 19327352832 | bytes 37748736 | tf_op jit(solution)/shard_map/dot_general | solution.py:41
  828.8 0.0 reduce-scatter.2.cloned.1.call-update
  828.9 0.0 copy-start.2
  828.9 31.3 %multiply_convert_fusion = bf16[6144,1536]{1,0:T(8,128)(2,1)} fusion(bf16[1024,1536]{1,0:T(8,128)(2,1)S(1)} %copy-done, bf16[1024,6144]{1,0:T(8,128)(2,1)} %param.6), kind=kOutput, calls=%fused_computation.7 | convolution fusion | flops 19409141760 | bytes 34603008 | tf_op jit(solution)/shard_map/dot_general | solution.py:31
  860.2 0.0 copy-done.2
  860.2 28.7 %fusion.11 = bf16[1536,6144]{0,1:T(8,128)(2,1)} fusion(bf16[1024,6144]{1,0:T(8,128)(2,1)} %copy-done.1, bf16[1024,1536]{1,0:T(8,128)(2,1)S(1)} %copy-done.2), kind=kOutput, calls=%fused_computation.20 | convolution fusion | flops 19346227200 | bytes 34603008 | tf_op jit(solution)/shard_map/dot_general | solution.py:38
  888.8 24.6 %copy.8 = bf16[1536,6144]{1,0:T(8,128)(2,1)} copy(bf16[1536,6144]{0,1:T(8,128)(2,1)} %fusion.11) | data formatting | bytes 37748736
  913.4 0.0 reduce-scatter.2.cloned.1.call-done
  913.4 2.4 convert_element_type.23
Async XLA Ops:
  7.2 1.9 copy-start
  7.2 772.8 %all-reduce.2.cloned.1.call-start = ((), (), s32[]{:S(2)}) async-start(), calls=%async_computation.1 | async-start | bytes 50331648 | tf_op jit(solution)/shard_map/psum | solution.py:36
  34.4 879.0 %reduce-scatter.2.cloned.1.call-start = ((), (), s32[]{:S(2)}) async-start(), calls=%async_computation.2 | async-start | bytes 7864320 | tf_op jit(solution)/shard_map/reduce_scatter | solution.py:45
  799.8 4.8 copy-start.1
  828.9 31.3 %copy-start.2 = (bf16[1024,1536]{1,0:T(8,128)(2,1)S(1)}, bf16[1024,1536]{1,0:T(8,128)(2,1)}, u32[]{:S(2)}) copy-start(bf16[1024,1536]{1,0:T(8,128)(2,1)} %param.5) | copy-start | bytes 9437188
Sparse Core Ops, SparseCore 0:
  34.6 745.4 all-reduce.1
  829.0 57.9 reduce-scatter.1
where the time goes:
time: 923 us
  waiting for transfers between devices  746 us (81%)
  matrix products  110 us (12%)
  local copies, waits for them, and re-layouts  31.2 us (3%)
  other arithmetic  22.1 us (2%)
  between operations  14.1 us (2%)
    psum x1, waiting for transfers between devices, body(): summed = lax.psum(local_sum, 'row')  746 us
    dot_general x1, matrix products, body(): lax.dot_general(activated, out_grad, CONTRACT_FIRST, preferred_element_ty...  31.3 us
    unnamed x7, local copies, waits for them, and re-layouts  31.2 us
    dot_general x1, matrix products, body(): lax.dot_general(layer_input, hidden_grad, CONTRACT_FIRST, preferred_eleme...  28.7 us
    dot_general x1, matrix products, body(): lax.dot_general(out_grad, w_down, CONTRACT_LAST, preferred_element_type=j...  25.3 us
    dot_general x1, matrix products, body(): lax.dot_general(hidden_grad, w_up, CONTRACT_LAST, preferred_element_type=...  24.3 us
    convert_element_type x1, other arithmetic, body(): hidden_grad = (summed * gelu_slope(pre_act)).astype(jnp.bfloat16)  19.7 us
  transfers between devices with their start and end apart: 2, of which 1 were waited for; matrix products, arithmetic and copies ran while one was open for 9% of the time, Pallas kernels for 0%

commit v1 on v0

--- a/solution.py
+++ b/solution.py
@@ -33,7 +33,9 @@
     )
     down_grad = (down_total * scaling).astype(jnp.bfloat16)
     local_sum = lax.dot_general(out_grad, w_down, CONTRACT_LAST, preferred_element_type=jnp.float32)
-    summed = lax.psum(local_sum, "row")
+    summed = local_sum
+    for hop in (1, 2, 4):
+        summed = summed + lax.ppermute(summed, "row", [(dev, dev ^ hop) for dev in range(8)])
     hidden_grad = (summed * gelu_slope(pre_act)).astype(jnp.bfloat16)
     up_total = lax.dot_general(
         layer_input, hidden_grad, CONTRACT_FIRST, preferred_element_type=jnp.float32

time: 923 us -> 2380 us (2.58)
  waiting for transfers between devices: 746 us -> 2160 us
  other arithmetic: 22.1 us -> 61.1 us
    ppermute x0 -> x3, waiting for transfers between devices: none -> 2160 us  [body(): lax.ppermute(summed, 'row', [(dev, dev ^ hop) for dev in range(8)])]
    psum x1 -> x0, waiting for transfers between devices: 746 us -> none  [body(): summed = lax.psum(local_sum, 'row')]
    add x0 -> x2, other arithmetic: none -> 34.5 us  [body(): summed + lax.ppermute(summed, 'row', [(dev, dev ^ hop) for dev in range(8)])]
  transfers between devices with their start and end apart: 2 -> 4, of which waited for: 1 -> 3; matrix products, arithmetic and copies ran while one was open for 9% -> 4% of each run, Pallas kernels for 0% -> 0%
where the time goes in v1:
time: 2380 us
  waiting for transfers between devices  2160 us (91%)
  matrix products  110 us (5%)
  other arithmetic  61.1 us (3%)
  local copies, waits for them, and re-layouts  31.2 us (1%)
    ppermute x3, waiting for transfers between devices, body(): lax.ppermute(summed, 'row', [(dev, dev ^ hop) for dev in range(8)])  2160 us
  transfers between devices with their start and end apart: 4, of which 3 were waited for; matrix products, arithmetic and copies ran while one was open for 4% of the time, Pallas kernels for 0%

profile of v1, /device:TPU:0, one launch (start us, length us, event | category | flops | bytes accessed | tf_op | source)
XLA Modules:
  0.0 2381.6 jit_solution(5070269307210259286)
XLA Ops:
  7.2 0.0 copy-start
  7.2 0.0 reduce-scatter.2.cloned.1.call-start
  7.2 1.8 copy-done
  9.1 25.4 %fusion.21 = f32[1024,6144]{1,0:T(8,128)} fusion(bf16[1024,1536]{1,0:T(8,128)(2,1)S(1)} %copy-done, bf16[6144,1536]{1,0:T(8,128)(2,1)} %param.9), kind=kOutput, calls=%fused_computation.29 | convolution fusion | flops 19327352832 | bytes 47185920 | tf_op jit(solution)/shard_map/dot_general | solution.py:35
  34.4 3.0 collective-permute-start
  37.4 540.3 %collective-permute-done = f32[1024,6144]{1,0:T(8,128)} collective-permute-done((f32[1024,6144]{1,0:T(8,128)}, f32[1024,6144]{1,0:T(8,128)}, u32[]{:S(2)}, u32[]{:S(2)}) %collective-permute-start) | collective-permute-done | bytes 25165856 | tf_op jit(solution)/shard_map/ppermute | solution.py:38
  577.7 16.4 add.25
  594.1 1.9 collective-permute-start.1
  596.0 539.4 %collective-permute-done.1 = f32[1024,6144]{1,0:T(8,128)} collective-permute-done((f32[1024,6144]{1,0:T(8,128)S(1)}, f32[1024,6144]{1,0:T(8,128)}, u32[]{:S(2)}, u32[]{:S(2)}) %collective-permute-start.1) | collective-permute-done | bytes 25165856 | tf_op jit(solution)/shard_map/ppermute | solution.py:38
  1135.5 18.1 add.26
  1153.6 2.5 collective-permute-start.2
  1156.1 1078.3 %collective-permute-done.2 = f32[1024,6144]{1,0:T(8,128)} collective-permute-done((f32[1024,6144]{1,0:T(8,128)}, f32[1024,6144]{1,0:T(8,128)}, u32[]{:S(2)}, u32[]{:S(2)}) %collective-permute-start.2) | collective-permute-done | bytes 25165856 | tf_op jit(solution)/shard_map/ppermute | solution.py:38
  2234.4 24.2 %fusion.6 = bf16[1024,6144]{1,0:T(8,128)(2,1)S(1)} fusion(bf16[1024,6144]{1,0:T(8,128)(2,1)} %param.6, f32[1024,6144]{1,0:T(8,128)} %add.26, f32[1024,6144]{1,0:T(8,128)} %collective-permute-done.2), kind=kLoop, calls=%fused_computation.15 | loop fusion | flops 132120576 | bytes 75497472 | tf_op jit(solution)/shard_map/convert_element_type | solution.py:39
  2258.6 0.0 copy-start.1
  2258.6 4.8 copy-done.1
  2263.4 24.3 %fusion.22 = f32[1024,1536]{1,0:T(8,128)} fusion(bf16[1024,6144]{1,0:T(8,128)(2,1)S(1)} %fusion.6, bf16[1536,6144]{1,0:T(8,128)(2,1)} %param.8), kind=kOutput, calls=%fused_computation.30 | convolution fusion | flops 19327352832 | bytes 37748736 | tf_op jit(solution)/shard_map/dot_general | solution.py:43
  2287.7 0.0 reduce-scatter.2.cloned.1.call-update
  2287.7 0.0 copy-start.2
  2287.7 31.4 %multiply_convert_fusion = bf16[6144,1536]{1,0:T(8,128)(2,1)} fusion(bf16[1024,1536]{1,0:T(8,128)(2,1)S(1)} %copy-done, bf16[1024,6144]{1,0:T(8,128)(2,1)} %param.6), kind=kOutput, calls=%fused_computation.7 | convolution fusion | flops 19409141760 | bytes 34603008 | tf_op jit(solution)/shard_map/dot_general | solution.py:31
  2319.1 0.0 copy-done.2
  2319.1 28.7 %fusion.11 = bf16[1536,6144]{0,1:T(8,128)(2,1)} fusion(bf16[1024,6144]{1,0:T(8,128)(2,1)} %copy-done.1, bf16[1024,1536]{1,0:T(8,128)(2,1)S(1)} %copy-done.2), kind=kOutput, calls=%fused_computation.20 | convolution fusion | flops 19346227200 | bytes 34603008 | tf_op jit(solution)/shard_map/dot_general | solution.py:40
  2347.8 24.6 %copy.8 = bf16[1536,6144]{1,0:T(8,128)(2,1)} copy(bf16[1536,6144]{0,1:T(8,128)(2,1)} %fusion.11) | data formatting | bytes 37748736
  2372.4 0.0 reduce-scatter.2.cloned.1.call-done
  2372.4 2.4 convert_element_type.23
Async XLA Ops:
  7.2 1.9 copy-start
  7.2 2365.2 %reduce-scatter.2.cloned.1.call-start = ((), (), s32[]{:S(2)}) async-start(), calls=%async_computation.1 | async-start | bytes 7864320 | tf_op jit(solution)/shard_map/reduce_scatter | solution.py:47
  34.4 543.3 %collective-permute-start = (f32[1024,6144]{1,0:T(8,128)}, f32[1024,6144]{1,0:T(8,128)}, u32[]{:S(2)}, u32[]{:S(2)}) collective-permute-start(f32[1024,6144]{1,0:T(8,128)} %fusion.21), channel_id=1, source_target_pairs={{0,4},{4,0},{8,12},{12,8},{16,20},{20,16},{24,28},{28,24},{1,5},{5... | collective-permute-start | bytes 75497480 | tf_op jit(solution)/shard_map/ppermute | solution.py:38
  594.1 541.3 %collective-permute-start.1 = (f32[1024,6144]{1,0:T(8,128)S(1)}, f32[1024,6144]{1,0:T(8,128)}, u32[]{:S(2)}, u32[]{:S(2)}) collective-permute-start(f32[1024,6144]{1,0:T(8,128)S(1)} %add.25), channel_id=1, source_target_pairs={{0,8},{4,12},{8,0},{12,4},{16,24},{20,28},{24,16},{28,20},{1,9},{5... | collective-permute-start | bytes 75497480 | tf_op jit(solution)/shard_map/ppermute | solution.py:38
  1153.6 1080.8 %collective-permute-start.2 = (f32[1024,6144]{1,0:T(8,128)}, f32[1024,6144]{1,0:T(8,128)}, u32[]{:S(2)}, u32[]{:S(2)}) collective-permute-start(f32[1024,6144]{1,0:T(8,128)} %add.26), channel_id=1, source_target_pairs={{0,16},{4,20},{8,24},{12,28},{16,0},{20,4},{24,8},{28,12},{1,17},{... | collective-permute-start | bytes 75497480 | tf_op jit(solution)/shard_map/ppermute | solution.py:38
  2258.6 4.8 copy-start.1
  2287.7 31.4 %copy-start.2 = (bf16[1024,1536]{1,0:T(8,128)(2,1)S(1)}, bf16[1024,1536]{1,0:T(8,128)(2,1)}, u32[]{:S(2)}) copy-start(bf16[1024,1536]{1,0:T(8,128)(2,1)} %param.5) | copy-start | bytes 9437188
Sparse Core Ops, SparseCore 0:
  2287.8 59.6 reduce-scatter.1
